TPU v7x, 256 devices: a whole 4x4x8 slice. The times are simulated.
256 devices in a mesh: row: 16 (over z, core), col: 8 (over x_hi, y), feat: 2 (over x_lo).
Axes of the slice: x: 4 (x_hi: 2, x_lo: 2; x = x_hi * 2 + x_lo), y: 4, z: 8, core: 2. Of those that a mesh axis runs over, the one named last changes fastest.
Arguments:
- features: bfloat16 [65536, 256], P(('col', 'row'), 'feat'), may hold values from -6 to 6
- tile_rows: int32 [16, 8, 256], P('row', 'col'), may hold values from 0 to 31, as said below
- tile_cols: int32 [16, 8, 256], P('row', 'col'), may hold values from 0 to 63
- tile_count: int32 [16, 8], P('row', 'col'), may hold values from 64 to 256, as said below
- tile_values: bfloat16 [16, 8, 256, 128, 128], P('row', 'col'), may hold values from -0.21875 to 0.21875
- weights: bfloat16 [256, 256], replicated, may hold values from -0.375 to 0.375
- cotangent: bfloat16 [65536, 256], P(('row', 'col'), 'feat'), may hold values from -6 to 6
Outputs:
- activated: bfloat16 [65536, 256], P(('row', 'col'), 'feat')
- feature_grad: bfloat16 [65536, 256], P(('col', 'row'), 'feat')
- weight_grad: float32 [256, 256], P('feat')
Inputs may be any that keep to these rules, and one draw needn't show every extreme that they name: `tile_rows`: block rows of a cell, unevenly loaded. `tile_count`: some cell has all 256 slots live.
All inputs are finite; a program needn't handle non-finite values.
Results may differ from a plain program's by a relative error of at most 0.027.
Values may be sent and summed in bfloat16 or wider, within the bound.
A program may use at most 128 MiB of HBM per device.

v0:
```python
import jax
import jax.numpy as jnp
from jax import lax
from jax.sharding import PartitionSpec as P


def shards(features, tile_rows, tile_cols, tile_count, tile_values, weights, cotangent):
    width = tile_values.shape[-1]
    slots = tile_values.shape[2]
    local_tiles = tile_values[0, 0]
    block_rows = tile_rows[0, 0]
    block_cols = tile_cols[0, 0]
    live_mask = (jnp.arange(slots) < tile_count[0, 0]).astype(jnp.float32)
    n_rowdev = lax.axis_size("row")
    n_coldev = lax.axis_size("col")
    local_blocks = features.shape[0] // width
    feat_half = features.shape[1]
    feat_index = lax.axis_index("feat")
    row_blocks = local_blocks * n_coldev
    col_blocks = local_blocks * n_rowdev
    node_total = features.shape[0] * n_rowdev * n_coldev
    panel = lax.all_gather(features, "row", axis=0, tiled=True)
    gathered = panel.reshape(col_blocks, width, feat_half)[block_cols]
    products = jnp.einsum("tij,tjf->tif", local_tiles, gathered, preferred_element_type=jnp.float32)
    products = products * live_mask[:, None, None]
    partial_value = (
        jnp.zeros((row_blocks, width, feat_half), jnp.float32).at[block_rows].add(products)
    )
    summed = lax.psum_scatter(
        partial_value.reshape(row_blocks * width, feat_half).astype(jnp.bfloat16),
        "col",
        scatter_dimension=0,
        tiled=True,
    )
    weight_rows = lax.dynamic_slice_in_dim(weights, feat_index * feat_half, feat_half, 0)
    mix_term = jnp.dot(summed, weight_rows, preferred_element_type=jnp.float32)
    hidden = lax.psum_scatter(
        mix_term.astype(jnp.bfloat16), "feat", scatter_dimension=1, tiled=True
    ).astype(jnp.float32)
    negative = jnp.minimum(hidden, 0.0)
    activated = jnp.where(hidden > 0, hidden, jnp.expm1(negative)).astype(jnp.bfloat16)
    slope_factor = jnp.where(hidden > 0, 1.0, jnp.exp(negative))
    grad_out = (cotangent.astype(jnp.float32) * slope_factor).astype(jnp.bfloat16)
    grad_whole = lax.all_gather(grad_out, "feat", axis=1, tiled=True)
    weight_term = lax.dot_general(
        summed, grad_whole, (((0,), (0,)), ((), ())), preferred_element_type=jnp.float32
    )
    n_feat = lax.axis_size("feat")
    slots = jnp.zeros((n_feat,) + weight_term.shape, jnp.float32)
    slots = lax.dynamic_update_slice_in_dim(slots, weight_term[None], feat_index, 0)
    slots = lax.psum(slots, ("row", "col", "feat"))
    weight_grad = lax.dynamic_index_in_dim(slots, feat_index, 0, keepdims=False) * node_total ** (
        -0.5
    )
    spread = lax.dot_general(
        grad_whole, weight_rows, (((1,), (1,)), ((), ())), preferred_element_type=jnp.float32
    ).astype(jnp.bfloat16)
    spread_panel = lax.all_gather(spread, "col", axis=0, tiled=True)
    spread_blocks = spread_panel.reshape(row_blocks, width, feat_half)[block_rows]
    back_products = jnp.einsum(
        "tji,tjf->tif", local_tiles, spread_blocks, preferred_element_type=jnp.float32
    )
    back_products = back_products * live_mask[:, None, None]
    back_partial = (
        jnp.zeros((col_blocks, width, feat_half), jnp.float32).at[block_cols].add(back_products)
    )
    back_summed = lax.psum_scatter(
        back_partial.reshape(col_blocks * width, feat_half).astype(jnp.bfloat16),
        "row",
        scatter_dimension=0,
        tiled=True,
    )
    return (activated, back_summed, weight_grad)


def solution(mesh):
    return jax.shard_map(
        shards,
        mesh=mesh,
        in_specs=(
            P(("col", "row"), "feat"),
            P("row", "col", None),
            P("row", "col", None),
            P("row", "col"),
            P("row", "col", None, None, None),
            P(),
            P(("row", "col"), "feat"),
        ),
        out_specs=(P(("row", "col"), "feat"), P(("col", "row"), "feat"), P("feat", None)),
        check_vma=False,
    )
```

profile of v0, /device:TPU:2, one launch (start us, length us, event | category | flops | bytes accessed | tf_op | source)
XLA Modules:
  0.0 605.1 jit_solution(15216501221385841070)
XLA Ops:
  7.2 0.0 copy-start
  7.2 0.0 all-gather.3.cloned.1.call-start
  7.2 0.7 all-gather.3.cloned.1.call-update
  7.9 0.0 reduce-scatter.6.cloned.1.call-start
  8.6 0.7 compare_select_fusion
  9.3 43.2 %all-gather.3.cloned.1.call-done = bf16[8192,128]{1,0:T(8,128)(2,1)} async-done(((bf16[512,128]{1,0:T(8,128)(2,1)}), bf16[8192,128]{1,0:T(8,128)(2,1)}) %all-gather.3.cloned.1.call-update) | async-done | bytes 2097168 | tf_op jit(solution)/shard_map/all_gather | solution.py:22
  52.6 10.2 %gather_fusion = bf16[256,128,128]{2,1,0:T(8,128)(2,1)} fusion(bf16[64,128,128]{2,1,0:T(8,128)(2,1)} %bitcast.36, s32[1024]{0:T(1024)S(1)} %pad_clamp_fusion.1), kind=kCustom, calls=%fused_computation | custom fusion | bytes 16778240 | tf_op jit(solution)/shard_map/gather | solution.py:23
  62.8 13.0 %multiply_bitcast_fusion.1 = f32[256,128,128]{1,2,0:T(8,128)} fusion(bf16[256,128,128]{2,1,0:T(8,128)(2,1)} %gather_fusion, bf16[1,1,256,128,128]{4,3,2,1,0:T(8,128)(2,1)} %param.11, f32[256]{0:T(256)S(1)} %compare_convert_fusion), kind=kOutput, calls=%fused_computation.5 | convolution fusion | flops 1077936128 | bytes 33555456 | tf_op jit(solution)/shard_map/tij,tjf->tif/dot_general | solution.py:24
  75.8 17.4 %copy.17 = f32[256,128,128]{2,1,0:T(8,128)} copy(f32[256,128,128]{1,2,0:T(8,128)} %multiply_bitcast_fusion.1) | data formatting | bytes 33554432 | tf_op jit(solution)/shard_map/mul | solution.py:25
  93.2 0.2 broadcast_in_dim.22
  93.5 0.0 copy-start.3
  93.5 33.2 %scatter_fusion = f32[32,128,128]{2,1,0:T(8,128)S(1)} fusion(f32[32,128,128]{2,1,0:T(8,128)S(1)} %broadcast_in_dim.22, s32[256]{0:T(256)S(1)} %bitcast.43, f32[256,128,128]{2,1,0:T(8,128)} %copy.17), kind=kCustom, calls=%fused_computation.2 | custom fusion | flops 4194304 | bytes 50332672 | tf_op jit(solution)/shard_map/scatter-add | solution.py:27
  126.7 1.1 convert_element_type.38
  127.8 0.0 reduce-scatter.6.cloned.1.call-update
  127.8 0.0 reduce-scatter.10.cloned.1.call-start
  127.9 74.5 %reduce-scatter.6.cloned.1.call-done = bf16[512,128]{1,0:T(8,128)(2,1)} async-done(((bf16[4096,128]{1,0:T(8,128)(2,1)}), bf16[512,128]{1,0:T(8,128)(2,1)}) %reduce-scatter.6.cloned.1.call-update) | async-done | bytes 131088 | tf_op jit(solution)/shard_map/reduce_scatter | solution.py:29
  202.3 0.0 copy-done
  202.4 1.1 convolution_convert_fusion
  203.5 0.8 copy.22
  204.3 0.0 reduce-scatter.10.cloned.1.call-update
  204.3 0.0 all-gather.5.cloned.1.call-start
  204.4 16.0 %reduce-scatter.10.cloned.1.call-done = bf16[128,512]{1,0:T(8,128)(2,1)} async-done(((bf16[256,512]{1,0:T(8,128)(2,1)}), bf16[128,512]{1,0:T(8,128)(2,1)}) %reduce-scatter.10.cloned.1.call-update) | async-done | bytes 131088
  220.4 1.0 copy.23
  221.4 0.0 copy-done.3
  221.5 0.8 fusion.7
  222.3 5.9 all_gather.10
  228.2 0.9 convolution_convert_fusion.1
  229.0 0.0 all-gather.5.cloned.1.call-update
  229.1 0.0 all-reduce.2.cloned.1.call-start
  229.2 1.1 fusion.2
  230.3 0.0 copy-start.2
  230.3 0.7 copy-done.2
  231.0 0.0 all-reduce.2.cloned.1.call-update
  231.0 0.2 reduce-scatter.8.cloned.1.call-start
  231.3 50.6 %all-gather.5.cloned.1.call-done = bf16[4096,128]{1,0:T(8,128)(2,1)} async-done(((bf16[512,128]{1,0:T(8,128)(2,1)}), bf16[4096,128]{1,0:T(8,128)(2,1)}) %all-gather.5.cloned.1.call-update) | async-done | bytes 1048592 | tf_op jit(solution)/shard_map/all_gather | solution.py:58
  281.9 9.8 %gather_fusion.1 = bf16[256,128,128]{2,1,0:T(8,128)(2,1)} fusion(bf16[32,128,128]{2,1,0:T(8,128)(2,1)} %bitcast.35, s32[1024]{0:T(1024)S(1)} %pad_clamp_fusion), kind=kCustom, calls=%fused_computation.1 | custom fusion | bytes 16778240 | tf_op jit(solution)/shard_map/gather | solution.py:59
  291.7 15.4 %multiply_bitcast_fusion = f32[256,128,128]{1,2,0:T(8,128)} fusion(bf16[256,128,128]{2,1,0:T(8,128)(2,1)} %gather_fusion.1, bf16[1,1,256,128,128]{4,3,2,1,0:T(8,128)(2,1)} %param.11, f32[256]{0:T(256)S(1)} %compare_convert_fusion), kind=kOutput, calls=%fused_computation.4 | convolution fusion | flops 1077936128 | bytes 33555456 | tf_op jit(solution)/shard_map/tji,tjf->tif/dot_general | solution.py:60
  307.1 17.5 %copy.19 = f32[256,128,128]{2,1,0:T(8,128)} copy(f32[256,128,128]{1,2,0:T(8,128)} %multiply_bitcast_fusion) | data formatting | bytes 33554432 | tf_op jit(solution)/shard_map/mul | solution.py:63
  324.6 2.5 broadcast_in_dim.23
  327.0 0.0 copy-start.1
  327.0 52.1 %scatter_fusion.1 = f32[64,128,128]{2,1,0:T(8,128)} fusion(f32[64,128,128]{2,1,0:T(8,128)} %broadcast_in_dim.23, s32[256]{0:T(256)S(1)} %bitcast.42, f32[256,128,128]{2,1,0:T(8,128)} %copy.19), kind=kCustom, calls=%fused_computation.3 | custom fusion | flops 4194304 | bytes 50332672 | tf_op jit(solution)/shard_map/scatter-add | solution.py:65
  379.1 3.9 convert_element_type.46
  383.0 0.0 reduce-scatter.8.cloned.1.call-update
  383.1 154.2 %all-reduce.2.cloned.1.call-done = f32[2,128,256]{2,1,0:T(8,128)} async-done(((f32[2,128,256]{2,1,0:T(8,128)}), f32[2,128,256]{2,1,0:T(8,128)}) %all-reduce.2.cloned.1.call-update) | async-done | bytes 262160 | tf_op jit(solution)/shard_map/psum | solution.py:51
  537.3 1.6 multiply_bitcast_fusion.2
  538.8 59.4 %reduce-scatter.8.cloned.1.call-done = bf16[512,128]{1,0:T(8,128)(2,1)} async-done(((bf16[8192,128]{1,0:T(8,128)(2,1)}), bf16[512,128]{1,0:T(8,128)(2,1)}) %reduce-scatter.8.cloned.1.call-update) | async-done | bytes 131088 | tf_op jit(solution)/shard_map/reduce_scatter | solution.py:67
  598.3 0.0 copy-done.1
  (4 shorter events, 0.0 us)
Async XLA Ops:
  7.2 195.2 %copy-start = (bf16[256,256]{1,0:T(8,128)(2,1)S(1)}, bf16[256,256]{1,0:T(8,128)(2,1)}, u32[]{:S(2)}) copy-start(bf16[256,256]{1,0:T(8,128)(2,1)} %param.12) | copy-start | bytes 393220
  7.2 45.4 %all-gather.3.cloned.1.call-start = ((), (), s32[]{:S(2)}) async-start(), calls=%async_computation.3 | async-start | bytes 2228224 | tf_op jit(solution)/shard_map/all_gather | solution.py:22
  7.9 194.4 %reduce-scatter.6.cloned.1.call-start = ((), (), s32[]{:S(2)}) async-start(), calls=%async_computation.4 | async-start | bytes 1179648 | tf_op jit(solution)/shard_map/reduce_scatter | solution.py:29
  93.5 128.0 %copy-start.3 = (bf16[512,128]{1,0:T(8,128)(2,1)S(1)}, bf16[512,128]{1,0:T(8,128)(2,1)}, u32[]{:S(2)}) copy-start(bf16[512,128]{1,0:T(8,128)(2,1)} %param.13) | copy-start | bytes 393220
  127.8 92.6 %reduce-scatter.10.cloned.1.call-start = ((), (), s32[]{:S(2)}) async-start(), calls=%async_computation.8 | async-start | bytes 393216
  204.3 77.5 %all-gather.5.cloned.1.call-start = ((), (), s32[]{:S(2)}) async-start(), calls=%async_computation.5 | async-start | bytes 1179648 | tf_op jit(solution)/shard_map/all_gather | solution.py:58
  229.1 308.2 %all-reduce.2.cloned.1.call-start = ((), (), s32[]{:S(2)}) async-start(), calls=%async_computation.7 | async-start | bytes 524288 | tf_op jit(solution)/shard_map/psum | solution.py:51
  230.3 0.7 copy-start.2
  231.0 367.2 %reduce-scatter.8.cloned.1.call-start = ((), (), s32[]{:S(2)}) async-start(), calls=%async_computation.6 | async-start | bytes 2228224 | tf_op jit(solution)/shard_map/reduce_scatter | solution.py:67
  327.0 271.2 %copy-start.1 = (bf16[256,256]{1,0:T(8,128)(2,1)S(1)}, bf16[256,256]{1,0:T(8,128)(2,1)}, u32[]{:S(2)}) copy-start(bf16[256,256]{1,0:T(8,128)(2,1)} %param.12) | copy-start | bytes 393220
Sparse Core Ops, SparseCore 0:
  9.8 42.6 all-gather.2
  127.9 74.3 reduce-scatter.5
  205.0 15.3 reduce-scatter.9
  229.2 52.6 all-gather.4
  287.2 250.0 all-reduce.1
  540.2 57.9 reduce-scatter.7
where the time goes:
time: 607 us; the launch traced here: 605 us
  waiting for transfers between devices  399 us (66%)
  other arithmetic  93.4 us (15%)
  local copies, waits for them, and re-layouts  60.2 us (10%)
  matrix products  31.5 us (5%)
  between operations  14.9 us (2%)
    psum x1, waiting for transfers between devices, shards(): slots = lax.psum(slots, ('row', 'col', 'feat'))  154 us
    reduce_scatter x1, waiting for transfers between devices, shards(): lax.psum_scatter(partial_value.reshape(row_blocks * width, feat_half).ast...  74.5 us
    reduce_scatter x1, waiting for transfers between devices, shards(): lax.psum_scatter(back_partial.reshape(col_blocks * width, feat_half).asty...  59.4 us
    scatter-add x1, other arithmetic, shards(): jnp.zeros((col_blocks, width, feat_half), jnp.float32).at[block_cols]  52.1 us
    all_gather x1, waiting for transfers between devices, shards(): spread_panel = lax.all_gather(spread, 'col', axis=0, tiled=True)  50.6 us
    all_gather x1, waiting for transfers between devices, shards(): panel = lax.all_gather(features, 'row', axis=0, tiled=True)  43.2 us
    scatter-add x1, other arithmetic, shards(): jnp.zeros((row_blocks, width, feat_half), jnp.float32).at[block_rows]  33.2 us
    mul x1, local copies, waits for them, and re-layouts, shards(): back_products = back_products * live_mask[:, None, None]  17.5 us
  transfers between devices with their start and end apart: 6, of which 6 were waited for; matrix products, arithmetic and copies ran while one was open for 17% of the time, Pallas kernels for 0%

commit v1 on v0

--- a/solution.py
+++ b/solution.py
@@ -2,6 +2,11 @@
 import jax.numpy as jnp
 from jax import lax
 from jax.sharding import PartitionSpec as P
+from jax.lax import all_to_all, psum
+
+
+def compute_view_here(a0):
+    return jnp.concatenate(all_to_all(jnp.stack([a0] * psum(1, "col")), "col", 0, 0), axis=0)
 
 
 def shards(features, tile_rows, tile_cols, tile_count, tile_values, weights, cotangent):
@@ -55,7 +60,7 @@
     spread = lax.dot_general(
         grad_whole, weight_rows, (((1,), (1,)), ((), ())), preferred_element_type=jnp.float32
     ).astype(jnp.bfloat16)
-    spread_panel = lax.all_gather(spread, "col", axis=0, tiled=True)
+    spread_panel = compute_view_here(spread)
     spread_blocks = spread_panel.reshape(row_blocks, width, feat_half)[block_rows]
     back_products = jnp.einsum(
         "tji,tjf->tif", local_tiles, spread_blocks, preferred_element_type=jnp.float32

time: 607 us -> 564 us (0.929)
  waiting for transfers between devices: 399 us -> 351 us
  starting transfers between devices: 0.42 us -> 6.76 us
    all_gather x1 -> x0, waiting for transfers between devices: 50.6 us -> none  [shards(): spread_panel = lax.all_gather(spread, 'col', axis=0, tiled=True)]
    all_to_all x0 -> x1, waiting for transfers between devices: none -> 12.8 us  [compute_view_here(): all_to_all(jnp.stack([a0] * psum(1, 'col')), 'col', 0, 0)]
    psum x1, waiting for transfers between devices: 154 us -> 145 us  [shards(): slots = lax.psum(slots, ('row', 'col', 'feat'))]
    all_to_all x0 -> x1, starting transfers between devices: none -> 6.38 us  [compute_view_here(): all_to_all(jnp.stack([a0] * psum(1, 'col')), 'col', 0, 0)]
    unnamed x7 -> x6, waiting for transfers between devices: 16.8 us -> 16.8 us
  transfers between devices with their start and end apart: 6 -> 6, of which waited for: 6 -> 6; matrix products, arithmetic and copies ran while one was open for 17% -> 18% of each run, Pallas kernels for 0% -> 0%
where the time goes in v1:
time: 564 us; the launch traced here: 563 us
  waiting for transfers between devices  351 us (62%)
  other arithmetic  92.9 us (16%)
  local copies, waits for them, and re-layouts  60.1 us (11%)
  matrix products  30.9 us (5%)
  between operations  14.5 us (3%)
  starting transfers between devices  6.76 us (1%)
  blocking collectives  5.91 us (1%)
    psum x1, waiting for transfers between devices, shards(): slots = lax.psum(slots, ('row', 'col', 'feat'))  145 us
    reduce_scatter x1, waiting for transfers between devices, shards(): lax.psum_scatter(partial_value.reshape(row_blocks * width, feat_half).ast...  74.4 us
    reduce_scatter x1, waiting for transfers between devices, shards(): lax.psum_scatter(back_partial.reshape(col_blocks * width, feat_half).asty...  59.4 us
    scatter-add x1, other arithmetic, shards(): jnp.zeros((col_blocks, width, feat_half), jnp.float32).at[block_cols]  51.6 us
    all_gather x1, waiting for transfers between devices, shards(): panel = lax.all_gather(features, 'row', axis=0, tiled=True)  43.2 us
    scatter-add x1, other arithmetic, shards(): jnp.zeros((row_blocks, width, feat_half), jnp.float32).at[block_rows]  33.2 us
    mul x1, local copies, waits for them, and re-layouts, shards(): back_products = back_products * live_mask[:, None, None]  17.5 us
    mul x1, local copies, waits for them, and re-layouts, shards(): products = products * live_mask[:, None, None]  17.5 us
  transfers between devices with their start and end apart: 6, of which 6 were waited for; matrix products, arithmetic and copies ran while one was open for 18% of the time, Pallas kernels for 0%

profile of v1, /device:TPU:2, one launch (start us, length us, event | category | flops | bytes accessed | tf_op | source)
XLA Modules:
  0.0 562.6 jit_solution(4470569831664324335)
XLA Ops:
  7.2 0.0 copy-start
  7.2 0.0 all-gather.2.cloned.1.call-start
  7.2 0.7 all-gather.2.cloned.1.call-update
  7.9 0.0 reduce-scatter.6.cloned.1.call-start
  8.6 0.7 compare_select_fusion
  9.3 43.2 %all-gather.2.cloned.1.call-done = bf16[8192,128]{1,0:T(8,128)(2,1)} async-done(((bf16[512,128]{1,0:T(8,128)(2,1)}), bf16[8192,128]{1,0:T(8,128)(2,1)}) %all-gather.2.cloned.1.call-update) | async-done | bytes 2097168 | tf_op jit(solution)/shard_map/all_gather | solution.py:27
  52.6 10.2 %gather_fusion = bf16[256,128,128]{2,1,0:T(8,128)(2,1)} fusion(bf16[64,128,128]{2,1,0:T(8,128)(2,1)} %bitcast.36, s32[1024]{0:T(1024)S(1)} %pad_clamp_fusion.1), kind=kCustom, calls=%fused_computation | custom fusion | bytes 16778240 | tf_op jit(solution)/shard_map/gather | solution.py:28
  62.8 13.0 %multiply_bitcast_fusion.1 = f32[256,128,128]{1,2,0:T(8,128)} fusion(bf16[256,128,128]{2,1,0:T(8,128)(2,1)} %gather_fusion, bf16[1,1,256,128,128]{4,3,2,1,0:T(8,128)(2,1)} %param.11, f32[256]{0:T(256)S(1)} %compare_convert_fusion), kind=kOutput, calls=%fused_computation.5 | convolution fusion | flops 1077936128 | bytes 33555456 | tf_op jit(solution)/shard_map/tij,tjf->tif/dot_general | solution.py:29
  75.8 17.5 %copy.17 = f32[256,128,128]{2,1,0:T(8,128)} copy(f32[256,128,128]{1,2,0:T(8,128)} %multiply_bitcast_fusion.1) | data formatting | bytes 33554432 | tf_op jit(solution)/shard_map/mul | solution.py:30
  93.2 0.2 broadcast_in_dim.22
  93.4 0.0 copy-start.3
  93.5 33.2 %scatter_fusion = f32[32,128,128]{2,1,0:T(8,128)S(1)} fusion(f32[32,128,128]{2,1,0:T(8,128)S(1)} %broadcast_in_dim.22, s32[256]{0:T(256)S(1)} %bitcast.43, f32[256,128,128]{2,1,0:T(8,128)} %copy.17), kind=kCustom, calls=%fused_computation.2 | custom fusion | flops 4194304 | bytes 50332672 | tf_op jit(solution)/shard_map/scatter-add | solution.py:32
  126.7 1.1 convert_element_type.38
  127.8 0.0 reduce-scatter.6.cloned.1.call-update
  127.8 0.0 reduce-scatter.10.cloned.1.call-start
  127.9 74.4 %reduce-scatter.6.cloned.1.call-done = bf16[512,128]{1,0:T(8,128)(2,1)} async-done(((bf16[4096,128]{1,0:T(8,128)(2,1)}), bf16[512,128]{1,0:T(8,128)(2,1)}) %reduce-scatter.6.cloned.1.call-update) | async-done | bytes 131088 | tf_op jit(solution)/shard_map/reduce_scatter | solution.py:34
  202.3 0.0 copy-done
  202.3 1.1 convolution_convert_fusion
  203.4 0.8 copy.22
  204.3 0.0 reduce-scatter.10.cloned.1.call-update
  204.3 16.1 %reduce-scatter.10.cloned.1.call-done = bf16[128,512]{1,0:T(8,128)(2,1)} async-done(((bf16[256,512]{1,0:T(8,128)(2,1)}), bf16[128,512]{1,0:T(8,128)(2,1)}) %reduce-scatter.10.cloned.1.call-update) | async-done | bytes 131088
  220.3 1.0 copy.23
  221.4 0.0 copy-done.3
  221.4 0.8 fusion.7
  222.2 5.9 %all_gather.7 = bf16[512,256]{1,0:T(8,128)(2,1)S(1)} all-gather(bf16[512,128]{1,0:T(8,128)(2,1)S(1)} %get-tuple-element.3), channel_id=1, replica_groups=mesh['row'=16,'col'=8,'feat'=2] {'feat'}, dimensions={1}, use_global_device_ids=true | all-gather | bytes 393216 | tf_op jit(solution)/shard_map/all_gather | solution.py:49
  228.1 0.2 convolution_convert_fusion.1
  228.3 1.1 stack.2
  229.4 6.4 %all-to-all-start = ((bf16[8,512,128]{2,1,0:T(8,128)(2,1)}), bf16[8,512,128]{2,1,0:T(8,128)(2,1)S(1)}, u32[]{:S(2)}, u32[]{:S(2)}) async-start(bf16[8,512,128]{2,1,0:T(8,128)(2,1)} %stack.2), calls=%async_computation.1 | async-start | bytes 2097152 | tf_op jit(solution)/shard_map/all_to_all | solution.py:9
  235.8 0.0 all-reduce.2.cloned.1.call-start
  235.9 1.1 fusion.2
  237.0 0.0 copy-start.2
  237.0 0.7 copy-done.2
  237.7 0.0 all-reduce.2.cloned.1.call-update
  237.8 0.2 reduce-scatter.8.cloned.1.call-start
  238.0 12.8 %all-to-all-done = bf16[8,512,128]{2,1,0:T(8,128)(2,1)S(1)} async-done(((bf16[8,512,128]{2,1,0:T(8,128)(2,1)}), bf16[8,512,128]{2,1,0:T(8,128)(2,1)S(1)}, u32[]{:S(2)}, u32[]{:S(2)}) %all-to-all-start) | async-done | bytes 1048608 | tf_op jit(solution)/shard_map/all_to_all | solution.py:9
  250.8 8.6 %gather_fusion.1 = bf16[256,128,128]{2,1,0:T(8,128)(2,1)} fusion(bf16[32,128,128]{2,1,0:T(8,128)(2,1)S(1)} %bitcast.35, s32[1024]{0:T(1024)S(1)} %pad_clamp_fusion), kind=kCustom, calls=%fused_computation.1 | custom fusion | bytes 16778240 | tf_op jit(solution)/shard_map/gather | solution.py:64
  259.4 15.5 %multiply_bitcast_fusion = f32[256,128,128]{1,2,0:T(8,128)} fusion(bf16[256,128,128]{2,1,0:T(8,128)(2,1)} %gather_fusion.1, bf16[1,1,256,128,128]{4,3,2,1,0:T(8,128)(2,1)} %param.11, f32[256]{0:T(256)S(1)} %compare_convert_fusion), kind=kOutput, calls=%fused_computation.4 | convolution fusion | flops 1077936128 | bytes 33555456 | tf_op jit(solution)/shard_map/tji,tjf->tif/dot_general | solution.py:65
  274.9 17.5 %copy.19 = f32[256,128,128]{2,1,0:T(8,128)} copy(f32[256,128,128]{1,2,0:T(8,128)} %multiply_bitcast_fusion) | data formatting | bytes 33554432 | tf_op jit(solution)/shard_map/mul | solution.py:68
  292.4 2.4 broadcast_in_dim.23
  294.8 0.0 copy-start.1
  294.8 51.6 %scatter_fusion.1 = f32[64,128,128]{2,1,0:T(8,128)} fusion(f32[64,128,128]{2,1,0:T(8,128)} %broadcast_in_dim.23, s32[256]{0:T(256)S(1)} %bitcast.42, f32[256,128,128]{2,1,0:T(8,128)} %copy.19), kind=kCustom, calls=%fused_computation.3 | custom fusion | flops 4194304 | bytes 50332672 | tf_op jit(solution)/shard_map/scatter-add | solution.py:70
  346.4 3.9 convert_element_type.46
  350.3 0.0 reduce-scatter.8.cloned.1.call-update
  350.3 144.7 %all-reduce.2.cloned.1.call-done = f32[2,128,256]{2,1,0:T(8,128)} async-done(((f32[2,128,256]{2,1,0:T(8,128)}), f32[2,128,256]{2,1,0:T(8,128)}) %all-reduce.2.cloned.1.call-update) | async-done | bytes 262160 | tf_op jit(solution)/shard_map/psum | solution.py:56
  495.0 1.6 multiply_bitcast_fusion.2
  496.6 59.4 %reduce-scatter.8.cloned.1.call-done = bf16[512,128]{1,0:T(8,128)(2,1)} async-done(((bf16[8192,128]{1,0:T(8,128)(2,1)}), bf16[512,128]{1,0:T(8,128)(2,1)}) %reduce-scatter.8.cloned.1.call-update) | async-done | bytes 131088 | tf_op jit(solution)/shard_map/reduce_scatter | solution.py:72
  556.0 0.0 copy-done.1
  (4 shorter events, 0.0 us)
Async XLA Ops:
  7.2 195.1 %copy-start = (bf16[256,256]{1,0:T(8,128)(2,1)S(1)}, bf16[256,256]{1,0:T(8,128)(2,1)}, u32[]{:S(2)}) copy-start(bf16[256,256]{1,0:T(8,128)(2,1)} %param.12) | copy-start | bytes 393220
  7.2 45.4 %all-gather.2.cloned.1.call-start = ((), (), s32[]{:S(2)}) async-start(), calls=%async_computation.4 | async-start | bytes 2228224 | tf_op jit(solution)/shard_map/all_gather | solution.py:27
  7.9 194.4 %reduce-scatter.6.cloned.1.call-start = ((), (), s32[]{:S(2)}) async-start(), calls=%async_computation.5 | async-start | bytes 1179648 | tf_op jit(solution)/shard_map/reduce_scatter | solution.py:34
  93.4 127.9 %copy-start.3 = (bf16[512,128]{1,0:T(8,128)(2,1)S(1)}, bf16[512,128]{1,0:T(8,128)(2,1)}, u32[]{:S(2)}) copy-start(bf16[512,128]{1,0:T(8,128)(2,1)} %param.13) | copy-start | bytes 393220
  127.8 92.5 %reduce-scatter.10.cloned.1.call-start = ((), (), s32[]{:S(2)}) async-start(), calls=%async_computation.8 | async-start | bytes 393216
  229.4 21.4 %all-to-all-start = ((bf16[8,512,128]{2,1,0:T(8,128)(2,1)}), bf16[8,512,128]{2,1,0:T(8,128)(2,1)S(1)}, u32[]{:S(2)}, u32[]{:S(2)}) async-start(bf16[8,512,128]{2,1,0:T(8,128)(2,1)} %stack.2), calls=%async_computation.1 | async-start | bytes 2097152 | tf_op jit(solution)/shard_map/all_to_all | solution.py:9
  235.8 259.2 %all-reduce.2.cloned.1.call-start = ((), (), s32[]{:S(2)}) async-start(), calls=%async_computation.7 | async-start | bytes 524288 | tf_op jit(solution)/shard_map/psum | solution.py:56
  237.0 0.7 copy-start.2
  237.8 318.3 %reduce-scatter.8.cloned.1.call-start = ((), (), s32[]{:S(2)}) async-start(), calls=%async_computation.6 | async-start | bytes 2228224 | tf_op jit(solution)/shard_map/reduce_scatter | solution.py:72
  294.8 261.2 %copy-start.1 = (bf16[256,256]{1,0:T(8,128)(2,1)S(1)}, bf16[256,256]{1,0:T(8,128)(2,1)}, u32[]{:S(2)}) copy-start(bf16[256,256]{1,0:T(8,128)(2,1)} %param.12) | copy-start | bytes 393220
Sparse Core Ops, SparseCore 0:
  9.8 42.6 all-gather.1
  127.9 74.3 reduce-scatter.5
  204.9 15.3 reduce-scatter.9
  241.8 253.2 all-reduce.1
  498.0 57.9 reduce-scatter.7
